TPU v7x, 32 devices: a whole 2x2x4 slice. The times are simulated.
32 devices in a mesh: group: 4 (over z), panel: 8 (over y, x, core).
Axes of the slice: x: 2, y: 2, z: 4, core: 2. Of those that a mesh axis runs over, the one named last changes fastest.
Arguments:
- source_matrix_tiles: bfloat16 [2, 48, 4, 4096], P(None, 'group', None, 'panel'), may hold values from -6 to 6
- second_operand_encoded: bfloat16 [32, 4096, 2, 4096], P('group', None, None, 'panel'), may hold values from -0.5 to 0.5
- responding_nodes: int32 [19], replicated, may hold values from 0 to 31, as said below
Outputs:
- c_blocks: float32 [2, 48, 2, 4096], P(None, 'group', None, 'panel')
Inputs may be any that keep to these rules, and one draw needn't show every extreme that they name: `responding_nodes`: 19 distinct point indices in ascending order; of the points 2 j and 2 j + 1, at least one is listed.
All inputs are finite; a program needn't handle non-finite values.
Results may differ from a plain program's by a relative error of at most 0.0029.
Values may be sent and summed in bfloat16 or wider, within the bound.
A program may use at most 192 MiB of HBM per device.

v0:
```python
import math

import jax
import jax.numpy as jnp
from jax import lax
from jax.sharding import PartitionSpec as P

NODE_NUMBER = 32


TWO_PI_RADIANS = 2.0 * math.pi


def point_trig(node_phases):
    exponent = (
        jnp.arange(4, dtype=jnp.float32)[None, :] + 8.0 * jnp.arange(2, dtype=jnp.float32)[:, None]
    )
    phase = node_phases[:, None, None] * exponent[None]
    return jnp.stack([jnp.cos(phase), jnp.sin(phase)], axis=1)


def recovery_coefficients(responding_nodes):
    responder_number = responding_nodes.shape[0]
    grid_index = jnp.arange(NODE_NUMBER, dtype=jnp.int32)
    grid_angle = TWO_PI_RADIANS * grid_index.astype(jnp.float32) / NODE_NUMBER
    node_angle = TWO_PI_RADIANS * responding_nodes.astype(jnp.float32) / NODE_NUMBER
    diff_real = jnp.cos(grid_angle)[None, :] - jnp.cos(node_angle)[:, None]
    diff_imag = jnp.sin(grid_angle)[None, :] - jnp.sin(node_angle)[:, None]
    ranks = jnp.arange(responder_number, dtype=jnp.int32)
    itself = (ranks[:, None] == ranks[None, :])[:, :, None]
    factor_real = jnp.where(itself, jnp.float32(1.0), diff_real[None])
    factor_imag = jnp.where(itself, jnp.float32(0.0), diff_imag[None])
    padded_width = 1 << (responder_number - 1).bit_length()
    extra = padded_width - responder_number
    factor_real = jnp.concatenate(
        [factor_real, jnp.ones((responder_number, extra, NODE_NUMBER), jnp.float32)], axis=1
    )
    factor_imag = jnp.concatenate(
        [factor_imag, jnp.zeros((responder_number, extra, NODE_NUMBER), jnp.float32)], axis=1
    )
    while factor_real.shape[1] > 1:
        middle = factor_real.shape[1] // 2
        left_real, right_real = (factor_real[:, :middle], factor_real[:, middle:])
        left_imag, right_imag = (factor_imag[:, :middle], factor_imag[:, middle:])
        factor_real = left_real * right_real - left_imag * right_imag
        factor_imag = left_real * right_imag + left_imag * right_real
    sample_real = factor_real[:, 0]
    sample_imag = factor_imag[:, 0]
    wanted = 3.0 + 4.0 * jnp.arange(4, dtype=jnp.float32)
    table_angle = -grid_angle[:, None] * wanted[None, :]
    table_cos = jnp.cos(table_angle)
    table_sin = jnp.sin(table_angle)
    highest = lax.Precision.HIGHEST
    numer_real = (
        jnp.dot(sample_real, table_cos, precision=highest)
        - jnp.dot(sample_imag, table_sin, precision=highest)
    ) / NODE_NUMBER
    numer_imag = (
        jnp.dot(sample_real, table_sin, precision=highest)
        + jnp.dot(sample_imag, table_cos, precision=highest)
    ) / NODE_NUMBER
    onehot = (responding_nodes[:, None] == grid_index[None, :]).astype(jnp.float32)
    denom_real = jnp.sum(onehot * sample_real, axis=1)
    denom_imag = jnp.sum(onehot * sample_imag, axis=1)
    magnitude = denom_real * denom_real + denom_imag * denom_imag
    coefficient_actual = (
        numer_real * denom_real[:, None] + numer_imag * denom_imag[:, None]
    ) / magnitude[:, None]
    coefficient_image = (
        numer_imag * denom_real[:, None] - numer_real * denom_imag[:, None]
    ) / magnitude[:, None]
    return (coefficient_actual, coefficient_image)


def weighted_slots(position_actual, position_image, real_part, imag_part):
    responder_number = position_actual.shape[0]
    output_matrix = jnp.einsum(
        "qil,qrn->irln",
        position_actual.reshape(responder_number, 2, 2),
        real_part,
        precision=lax.Precision.HIGHEST,
    )
    return output_matrix - jnp.einsum(
        "qil,qrn->irln",
        position_image.reshape(responder_number, 2, 2),
        imag_part,
        precision=lax.Precision.HIGHEST,
    )


def shards(source_matrix_tiles, second_operand_encoded, responding_nodes):
    coefficient_actual, coefficient_image = recovery_coefficients(responding_nodes)
    here = second_operand_encoded.shape[0]
    quarter = second_operand_encoded.shape[1]
    half_local = second_operand_encoded.shape[3]
    point_selector = (
        responding_nodes[:, None] == jnp.arange(NODE_NUMBER, dtype=jnp.int32)[None, :]
    ).astype(jnp.float32)
    every_real = jnp.dot(point_selector.T, coefficient_actual, precision=lax.Precision.HIGHEST)
    every_imag = jnp.dot(point_selector.T, coefficient_image, precision=lax.Precision.HIGHEST)
    first_point = lax.axis_index("group") * here
    local_real = lax.dynamic_slice_in_dim(every_real, first_point, here, 0)
    local_imag = lax.dynamic_slice_in_dim(every_imag, first_point, here, 0)
    shares_flat = second_operand_encoded.reshape(here, quarter, 2 * half_local)
    trig_every = point_trig(
        TWO_PI_RADIANS * jnp.arange(NODE_NUMBER, dtype=jnp.float32) / NODE_NUMBER
    )
    coded_every = jnp.einsum(
        "irkn,qcik->qcrn",
        source_matrix_tiles.astype(jnp.float32),
        trig_every,
        precision=lax.Precision.HIGHEST,
    ).astype(jnp.bfloat16)
    coded_here = lax.all_to_all(coded_every, "group", split_axis=0, concat_axis=2, tiled=True)
    products = jnp.einsum(
        "qcrk,qkn->qcrn",
        lax.all_gather(coded_here, "panel", axis=3, tiled=True),
        shares_flat,
        preferred_element_type=jnp.float32,
    )
    real_part = products[:, 0, :, :half_local] - products[:, 1, :, half_local:]
    imag_part = products[:, 0, :, half_local:] + products[:, 1, :, :half_local]
    partial_sum = weighted_slots(local_real, local_imag, real_part, imag_part)
    return lax.psum_scatter(partial_sum, "group", scatter_dimension=1, tiled=True)


def solution(mesh):
    placed = (P(None, "group", None, "panel"), P("group", None, None, "panel"), P())
    return jax.shard_map(
        shards,
        mesh=mesh,
        in_specs=placed,
        out_specs=P(None, "group", None, "panel"),
        check_vma=False,
    )
```

profile of v0, /device:TPU:0, one launch (start us, length us, event | category | flops | bytes accessed | tf_op | source)
XLA Modules:
  0.0 220.2 jit_solution(14585651845196669867)
XLA Ops:
  6.5 0.0 all-gather.2.cloned.1.call-start
  6.6 0.1 iota_add_fusion
  6.6 0.1 multiply_cosine_fusion.3
  6.8 1.8 bitcast_convert_fusion
  8.5 0.8 copy.38
  9.3 26.3 %all_to_all.18 = bf16[32,2,12,512]{3,1,2,0:T(2,128)(2,1)S(1)} all-to-all(bf16[32,2,12,512]{3,1,2,0:T(2,128)(2,1)S(1)} %copy.38), channel_id=1, replica_groups=mesh['group'=4,'panel'=8] {'group'}, dimensions={0} | all-to-all | bytes 1572864 | tf_op jit(solution)/shard_map/all_to_all | solution.py:114
  35.6 0.2 copy.63
  35.8 0.1 copy.40
  35.9 1.1 copy.41
  37.0 0.0 all-gather.2.cloned.1.call-update
  37.0 0.0 all-reduce.5.cloned.1.call-start
  37.1 0.0 copy-start
  37.1 106.3 %reshape.149 = bf16[8,4096,1024,1]{2,1,0,3:T(8,128)(2,1)} reshape(bf16[8,4096,2,512]{3,2,1,0:T(2,128)(2,1)} %param.4) | data formatting | bytes 134217728 | tf_op jit(solution)/shard_map/reshape | solution.py:104
  143.5 0.0 copy-done
  143.5 0.1 broadcast_subtract_fusion
  143.6 0.1 broadcast_select_fusion.1
  143.9 0.2 fusion.17
  144.1 0.3 fusion.11
  144.4 0.3 fusion.10
  144.7 0.3 convolution_subtract_fusion.1
  145.1 0.3 convolution_add_fusion
  145.4 0.2 fusion.19
  145.6 0.1 constant_dynamic-slice_fusion.2
  145.7 0.2 fusion.18
  145.9 0.1 constant_dynamic-slice_fusion.1
  146.0 0.0 all-gather.2.cloned.1.call-done
  146.0 25.0 %fusion = f32[8,2,48,1024]{3,2,1,0:T(8,128)S(1)} fusion(bf16[8,2,48,4096]{3,2,1,0:T(8,128)(2,1)} %all-gather.2.cloned.1.call-done, bf16[8,4096,1024,1]{2,1,0,3:T(8,128)(2,1)} %reshape.149), kind=kOutput, calls=%fused_computation | convolution fusion | flops 6442450944 | bytes 76546048 | tf_op jit(solution)/shard_map/qcrk,qkn->qcrn/dot_general | solution.py:115
  171.0 0.0 copy-start.1
  171.0 0.3 fusion.3
  171.4 1.7 fusion.6
  173.1 2.5 %fusion.2 = f32[2,48,2,512]{3,2,0,1:T(2,128)} fusion(f32[48,512,2,2]{1,3,2,0:T(2,128)S(1)} %fusion.6, f32[8,2,2,1]{0,2,1,3:T(2,128)S(1)} %bitcast.59, f32[8,48,512,1]{2,1,0,3:T(8,128)S(1)} %get-tuple-element.9), kind=kOutput, calls=%fused_computation.4 | convolution fusion | flops 9535488 | bytes 1572992 | tf_op jit(solution)/shard_map/qil,qrn->irln/dot_general | solution.py:83
  175.6 0.0 all-reduce.5.cloned.1.call-update
  175.6 0.0 copy-done.1
  175.6 0.6 dynamic-slice
  176.9 35.0 %all-reduce.5.cloned.1.call-done = f32[2,48,2,512]{3,2,0,1:T(2,128)} async-done(((f32[2,48,2,512]{3,2,0,1:T(2,128)}), f32[2,48,2,512]{3,2,0,1:T(2,128)}) %all-reduce.5.cloned.1.call-update) | async-done | bytes 393232
  211.8 0.9 constant_dynamic-slice_fusion
  212.7 0.6 copy.44
  (13 shorter events, 0.3 us)
Async XLA Ops:
  6.5 139.4 %all-gather.2.cloned.1.call-start = ((), (), s32[]{:S(2)}) async-start(), calls=%async_computation.1 | async-start | bytes 7077888 | tf_op jit(solution)/shard_map/all_gather | solution.py:117
  37.0 174.8 %all-reduce.5.cloned.1.call-start = ((), (), s32[]{:S(2)}) async-start(), calls=%async_computation.2 | async-start | bytes 786432
  37.1 106.4 %copy-start = (s32[19]{0:T(128)S(1)}, s32[19]{0:T(128)}, u32[]{:S(2)}) copy-start(s32[19]{0:T(128)} %param.5) | copy-start | bytes 232
  171.0 4.6 %copy-start.1 = (u32[32]{0:T(128)S(1)}, u32[32]{0:T(128)}, u32[]{:S(2)}) copy-start(u32[32]{0:T(128)} %constant.46) | copy-start | bytes 388
Sparse Core Ops, SparseCore 0:
  37.2 45.6 all-gather.1
  175.7 36.0 all-reduce.4
where the time goes:
time: 223 us; the launch traced here: 220 us
  local copies, waits for them, and re-layouts  111 us (50%)
  waiting for transfers between devices  35 us (16%)
  matrix products  32.7 us (15%)
  blocking collectives  26.3 us (12%)
  between operations  14.2 us (6%)
    reshape x1, local copies, waits for them, and re-layouts, shards(): shares_flat = second_operand_encoded.reshape(here, quarter, 2 * half_local)  106 us
    unnamed x3, waiting for transfers between devices  35 us
    all_to_all x1, blocking collectives, shards(): lax.all_to_all(coded_every, 'group', split_axis=0, concat_axis=2, tiled=T...  26.3 us
    dot_general x1, matrix products, shards(): jnp.einsum('qcrk,qkn->qcrn', lax.all_gather(coded_here, 'panel', axis=3,...  25 us
  transfers between devices with their start and end apart: 2, of which 1 were waited for; matrix products, arithmetic and copies ran while one was open for 50% of the time, Pallas kernels for 0%

commit v1 on v0

--- a/solution.py
+++ b/solution.py
@@ -1,14 +1,17 @@
+import functools
 import math
 
 import jax
 import jax.numpy as jnp
 from jax import lax
+from jax.experimental import pallas as pl
+from jax.experimental.pallas import tpu as pltpu
 from jax.sharding import PartitionSpec as P
 
 NODE_NUMBER = 32
-
-
 TWO_PI_RADIANS = 2.0 * math.pi
+LANES = 128
+DEPTH = 12
 
 
 def point_trig(node_phases):
@@ -72,55 +75,137 @@
     return (coefficient_actual, coefficient_image)
 
 
-def weighted_slots(position_actual, position_image, real_part, imag_part):
-    responder_number = position_actual.shape[0]
-    output_matrix = jnp.einsum(
-        "qil,qrn->irln",
-        position_actual.reshape(responder_number, 2, 2),
-        real_part,
-        precision=lax.Precision.HIGHEST,
-    )
-    return output_matrix - jnp.einsum(
-        "qil,qrn->irln",
-        position_image.reshape(responder_number, 2, 2),
-        imag_part,
-        precision=lax.Precision.HIGHEST,
-    )
+def product_kernel(
+    count_ref, order_ref, trig_ref, weight_ref, a_ref, spread_ref, b_ref, out_ref, buf, acc, sems
+):
+    rows, inner = a_ref.shape[1], a_ref.shape[2]
+    tiles = b_ref.shape[2]
+    depth, _, kb = buf.shape[0], buf.shape[1], buf.shape[2]
+    blocks = inner // kb
+    total = count_ref[0] * blocks
+
+    def copies(step):
+        point = order_ref[step // blocks]
+        start = pl.multiple_of((step % blocks) * kb, kb)
+        slot = step % depth
+        return [
+            pltpu.make_async_copy(
+                b_ref.at[point, pl.ds(start, kb), t], buf.at[slot, t], sems.at[slot, t]
+            )
+            for t in range(tiles)
+        ]
+
+    def fetch(step):
+        @pl.when(step < total)
+        def _():
+            for copy in copies(step):
+                copy.start()
+
+    for step in range(depth - 1):
+        fetch(step)
+    out_ref[...] = jnp.zeros_like(out_ref)
+
+    def body(step, carry):
+        fetch(step + depth - 1)
+        point = order_ref[step // blocks]
+        block = step % blocks
+        start = pl.multiple_of(block * kb, kb)
+        real = jnp.zeros((rows, kb), jnp.float32)
+        imag = jnp.zeros((rows, kb), jnp.float32)
+        for e in range(a_ref.shape[0]):
+            piece = a_ref[e, :, pl.ds(start, kb)].astype(jnp.float32)
+            real = real + piece * trig_ref[point, e]
+            imag = imag + piece * trig_ref[point, a_ref.shape[0] + e]
+        real = real.astype(jnp.bfloat16)
+        imag = imag.astype(jnp.bfloat16)
+        parts = []
+        for t in range(kb // LANES):
+            r = real[:, t * LANES : (t + 1) * LANES]
+            i = imag[:, t * LANES : (t + 1) * LANES]
+            parts.append(jnp.concatenate([r, -i], axis=1))
+            parts.append(jnp.concatenate([i, r], axis=1))
+        mixed = jnp.dot(
+            jnp.concatenate(parts, axis=0), spread_ref[...], preferred_element_type=jnp.float32
+        ).astype(jnp.bfloat16)
+        left = jnp.concatenate(
+            [mixed[2 * rows * t : 2 * rows * (t + 1)] for t in range(kb // LANES)], axis=1
+        )
+        for copy in copies(step):
+            copy.wait()
+        slot = step % depth
+        right = jnp.concatenate(
+            [buf[slot, t].reshape(2 * kb, LANES) for t in range(tiles)], axis=1
+        )
+        product = jnp.dot(left, right, preferred_element_type=jnp.float32)
+        value = jnp.where(block == 0, product, acc[...] + product)
+        acc[...] = value
+
+        @pl.when(block == blocks - 1)
+        def _():
+            for e in range(4):
+                out_ref[e] += (
+                    weight_ref[point, e] * value[:rows] - weight_ref[point, 4 + e] * value[rows:]
+                )
+
+        return carry
+
+    lax.fori_loop(0, total, body, 0)
+
+
+def weighted_product(count, order, trig, weight, whole, shares):
+    here, inner, tiles = shares.shape[0], shares.shape[1], shares.shape[2]
+    rows = whole.shape[1]
+    kb = min(inner, 512)
+    index = jnp.arange(2 * LANES)
+    target = jnp.where(index < LANES, 2 * index, 2 * (index - LANES) + 1)
+    spread = (target[:, None] == index[None, :]).astype(jnp.bfloat16)
+    smem = pl.BlockSpec(memory_space=pltpu.SMEM)
+    vmem = pl.BlockSpec(memory_space=pltpu.VMEM)
+    return pl.pallas_call(
+        product_kernel,
+        out_shape=jax.ShapeDtypeStruct((4, rows, tiles * LANES), jnp.float32),
+        in_specs=[smem, smem, smem, smem, vmem, vmem, pl.BlockSpec(memory_space=pl.ANY)],
+        out_specs=vmem,
+        scratch_shapes=[
+            pltpu.VMEM((DEPTH, tiles, kb, 2, LANES), jnp.bfloat16),
+            pltpu.VMEM((2 * rows, tiles * LANES), jnp.float32),
+            pltpu.SemaphoreType.DMA((DEPTH, tiles)),
+        ],
+        compiler_params=pltpu.CompilerParams(vmem_limit_bytes=50 << 20),
+    )(count, order, trig, weight, whole, spread, shares)
 
 
 def shards(source_matrix_tiles, second_operand_encoded, responding_nodes):
     coefficient_actual, coefficient_image = recovery_coefficients(responding_nodes)
-    here = second_operand_encoded.shape[0]
-    quarter = second_operand_encoded.shape[1]
-    half_local = second_operand_encoded.shape[3]
-    point_selector = (
-        responding_nodes[:, None] == jnp.arange(NODE_NUMBER, dtype=jnp.int32)[None, :]
-    ).astype(jnp.float32)
-    every_real = jnp.dot(point_selector.T, coefficient_actual, precision=lax.Precision.HIGHEST)
-    every_imag = jnp.dot(point_selector.T, coefficient_image, precision=lax.Precision.HIGHEST)
+    here, inner, _, cols = second_operand_encoded.shape
     first_point = lax.axis_index("group") * here
-    local_real = lax.dynamic_slice_in_dim(every_real, first_point, here, 0)
-    local_imag = lax.dynamic_slice_in_dim(every_imag, first_point, here, 0)
-    shares_flat = second_operand_encoded.reshape(here, quarter, 2 * half_local)
-    trig_every = point_trig(
-        TWO_PI_RADIANS * jnp.arange(NODE_NUMBER, dtype=jnp.float32) / NODE_NUMBER
-    )
-    coded_every = jnp.einsum(
-        "irkn,qcik->qcrn",
-        source_matrix_tiles.astype(jnp.float32),
-        trig_every,
-        precision=lax.Precision.HIGHEST,
-    ).astype(jnp.bfloat16)
-    coded_here = lax.all_to_all(coded_every, "group", split_axis=0, concat_axis=2, tiled=True)
-    products = jnp.einsum(
-        "qcrk,qkn->qcrn",
-        lax.all_gather(coded_here, "panel", axis=3, tiled=True),
-        shares_flat,
-        preferred_element_type=jnp.float32,
-    )
-    real_part = products[:, 0, :, :half_local] - products[:, 1, :, half_local:]
-    imag_part = products[:, 0, :, half_local:] + products[:, 1, :, :half_local]
-    partial_sum = weighted_slots(local_real, local_imag, real_part, imag_part)
+    points = first_point + jnp.arange(here, dtype=jnp.int32)
+    selector = (responding_nodes[:, None] == points[None, :]).astype(jnp.float32)
+    highest = lax.Precision.HIGHEST
+    weight = jnp.concatenate(
+        [
+            jnp.dot(selector.T, coefficient_actual, precision=highest),
+            jnp.dot(selector.T, coefficient_image, precision=highest),
+        ],
+        axis=1,
+    )
+    listed = jnp.any(responding_nodes[:, None] == points[None, :], axis=0)
+    rank = jnp.cumsum(listed.astype(jnp.int32)) - 1
+    local = jnp.arange(here, dtype=jnp.int32)
+    order = jnp.sum(
+        jnp.where(listed[None, :] & (rank[None, :] == local[:, None]), local[None, :], 0), axis=1
+    )
+    count = jnp.sum(listed.astype(jnp.int32))[None]
+    trig = point_trig(TWO_PI_RADIANS * points.astype(jnp.float32) / NODE_NUMBER)
+    trig = trig.reshape(here, 16)
+    whole = lax.all_gather(source_matrix_tiles, "group", axis=1, tiled=True)
+    whole = lax.all_gather(whole, "panel", axis=3, tiled=True)
+    rows = whole.shape[1]
+    whole = whole.transpose(0, 2, 1, 3).reshape(8, rows, inner)
+    shares = second_operand_encoded.reshape(here, inner, 2, cols // LANES, LANES)
+    shares = shares.transpose(0, 1, 3, 2, 4)
+    partial_sum = weighted_product(count, order, trig, weight, whole, shares)
+    partial_sum = partial_sum.reshape(2, 2, rows, cols).transpose(0, 2, 1, 3)
     return lax.psum_scatter(partial_sum, "group", scatter_dimension=1, tiled=True)
 
 

time: 223 us -> 156 us (0.70)
  local copies, waits for them, and re-layouts: 111 us -> 6.87 us
  waiting for transfers between devices: 35 us -> 77.6 us
  Pallas kernels: 0 us -> 33.2 us
  matrix products: 32.7 us -> 1.72 us
  blocking collectives: 26.3 us -> 18.4 us
  other arithmetic: 1.19 us -> 3.5 us
    reshape x1 -> x2, local copies, waits for them, and re-layouts: 106 us -> 1.12 us  [the longest x1 1.05 us: shards(): partial_sum = partial_sum.reshape(2, 2, rows, cols).transpose(0, 2, 1, 3)]
    pallas_call x0 -> x1, Pallas kernels: none -> 33.2 us  [weighted_product(): pl.pallas_call(product_kernel, out_shape=jax.ShapeDtypeStruct((4, rows, t...]
    dot_general x6 -> x2, matrix products: 31.4 us -> 0.38 us  [the longest x1 0.19 us: shards(): jnp.dot(selector.T, coefficient_image, precision=highest)]
    all_gather x1, waiting for transfers between devices: 0.01 us -> 27.3 us  [shards(): whole = lax.all_gather(whole, 'panel', axis=3, tiled=True)]
    all_to_all x1 -> x0, blocking collectives: 26.3 us -> none  [shards(): lax.all_to_all(coded_every, 'group', split_axis=0, concat_axis=2, tiled=T...]
    all_gather x0 -> x1, blocking collectives: none -> 18.4 us  [shards(): whole = lax.all_gather(source_matrix_tiles, 'group', axis=1, tiled=True)]
    unnamed x3, waiting for transfers between devices: 35 us -> 50.2 us
    transpose x0 -> x1, local copies, waits for them, and re-layouts: none -> 3.61 us  [shards(): whole = whole.transpose(0, 2, 1, 3).reshape(8, rows, inner)]
  transfers between devices with their start and end apart: 2 -> 2, of which waited for: 1 -> 2; matrix products, arithmetic and copies ran while one was open for 50% -> 4% of each run, Pallas kernels for 0% -> 0%
where the time goes in v1:
time: 156 us; the launch traced here: 155 us
  waiting for transfers between devices  77.6 us (50%)
  Pallas kernels  33.2 us (21%)
  blocking collectives  18.4 us (12%)
  between operations  14.2 us (9%)
  local copies, waits for them, and re-layouts  6.87 us (4%)
  other arithmetic  3.5 us (2%)
  matrix products  1.72 us (1%)
    unnamed x3, waiting for transfers between devices  50.2 us
    pallas_call x1, Pallas kernels, weighted_product(): pl.pallas_call(product_kernel, out_shape=jax.ShapeDtypeStruct((4, rows, t...  33.2 us
    all_gather x1, waiting for transfers between devices, shards(): whole = lax.all_gather(whole, 'panel', axis=3, tiled=True)  27.3 us
    all_gather x1, blocking collectives, shards(): whole = lax.all_gather(source_matrix_tiles, 'group', axis=1, tiled=True)  18.4 us
    transpose x1, local copies, waits for them, and re-layouts, shards(): whole = whole.transpose(0, 2, 1, 3).reshape(8, rows, inner)  3.61 us
  transfers between devices with their start and end apart: 2, of which 2 were waited for; matrix products, arithmetic and copies ran while one was open for 4% of the time, Pallas kernels for 0%

profile of v1, /device:TPU:0, one launch (start us, length us, event | category | flops | bytes accessed | tf_op | source)
XLA Modules:
  0.0 155.4 jit_solution(6043842896053493063)
XLA Ops:
  6.5 0.0 copy-start
  6.5 0.0 all-gather.2.cloned.1.call-start
  6.5 18.4 %all_gather.6 = bf16[2,48,4,512]{3,2,1,0:T(4,128)(2,1)} all-gather(bf16[2,12,4,512]{3,2,1,0:T(4,128)(2,1)} %param.3), channel_id=1, replica_groups=mesh['group'=4,'panel'=8] {'group'}, dimensions={1}, use_global_device_ids=true | all-gather | bytes 491520 | tf_op jit(solution)/shard_map/all_gather | solution.py:201
  24.9 0.0 all-gather.2.cloned.1.call-update
  25.0 0.0 all-reduce.5.cloned.1.call-start
  25.0 0.1 iota_add_fusion.1
  25.1 0.1 multiply_cosine_fusion.3
  25.3 0.1 copy.59.trig_ref
  25.3 0.8 compare_reduce_fusion
  26.2 0.2 reduce-window.8
  26.5 0.6 convert_reduce_fusion
  27.1 0.7 fusion.47
  27.8 0.1 broadcast_subtract_fusion
  27.9 0.1 broadcast_select_fusion.1
  28.2 0.0 copy-done
  28.2 0.2 fusion.8
  28.4 0.3 fusion.2
  28.7 0.3 fusion.1
  29.0 0.4 convolution_add_fusion
  29.4 0.3 convolution_subtract_fusion
  29.7 0.2 fusion.19
  29.9 0.2 fusion.17
  30.1 0.1 pad_maximum_fusion.1.weight_ref
  30.2 0.1 select_reduce_fusion.order_ref
  30.3 0.1 fusion.spread_ref
  30.4 27.3 %all-gather.2.cloned.1.call-done = bf16[2,48,4,4096]{3,2,1,0:T(4,128)(2,1)} async-done(((bf16[2,48,4,512]{3,2,1,0:T(4,128)(2,1)}), bf16[2,48,4,4096]{3,2,1,0:T(4,128)(2,1)}) %all-gather.2.cloned.1.call-update) | async-done | bytes 3145744 | tf_op jit(solution)/shard_map/all_gather | solution.py:202
  57.8 3.6 %copy.58 = bf16[2,4,48,4096]{3,2,1,0:T(8,128)(2,1)S(1)} copy(bf16[2,4,48,4096]{3,1,2,0:T(4,128)(2,1)} %bitcast.36) | data formatting | bytes 6291456 | tf_op jit(solution)/shard_map/transpose | solution.py:204
  61.4 0.0 copy-start.1
  61.4 33.2 %shard_map.37 = f32[4,48,512]{2,1,0:T(8,128)S(1)} custom-call(s32[1]{0:T(128)} %bitcast.count_ref, s32[8]{0:T(128)S(1)} %select_reduce_fusion.order_ref, f32[8,16]{1,0:T(8,128)S(1)} %copy.59.trig_ref, f32[8,8]{1,0:T(8,128)S(1)} %pad_maximum_fusion.1.weight_ref, bf16[8,48,4096]{2,1,0:T(8,128)(2,1)S(1)} %bitcast.34, bf16[256,256]{1,0:T(8,128)(2,1)S(1)} %fusion.spread_ref, ...), custom_call_target="tpu_custom_call" | custom-call | tf_op jit(solution)/shard_map/pallas_call | solution.py:164
  94.5 1.1 copy.66
  95.6 0.0 all-reduce.5.cloned.1.call-update
  95.6 0.0 copy-done.1
  95.6 0.6 dynamic-slice
  96.9 50.2 %all-reduce.5.cloned.1.call-done = f32[2,48,2,512]{3,2,1,0:T(2,128)} async-done(((f32[2,48,2,512]{3,2,1,0:T(2,128)}), f32[2,48,2,512]{3,2,1,0:T(2,128)}) %all-reduce.5.cloned.1.call-update) | async-done | bytes 393232
  147.1 1.5 constant_dynamic-slice_fusion
  (17 shorter events, 0.3 us)
Async XLA Ops:
  6.5 21.6 %copy-start = (s32[19]{0:T(128)S(1)}, s32[19]{0:T(128)}, u32[]{:S(2)}) copy-start(s32[19]{0:T(128)} %param.5) | copy-start | bytes 232
  6.5 51.2 %all-gather.2.cloned.1.call-start = ((), (), s32[]{:S(2)}) async-start(), calls=%async_computation | async-start | bytes 3538944 | tf_op jit(solution)/shard_map/all_gather | solution.py:202
  25.0 122.1 %all-reduce.5.cloned.1.call-start = ((), (), s32[]{:S(2)}) async-start(), calls=%async_computation.1 | async-start | bytes 786432
  61.4 34.3 %copy-start.1 = (u32[32]{0:T(128)S(1)}, u32[32]{0:T(128)}, u32[]{:S(2)}) copy-start(u32[32]{0:T(128)} %constant.62) | copy-start | bytes 388
Sparse Core Ops, SparseCore 0:
  25.1 32.6 all-gather.1
  95.7 51.2 all-reduce.4

commit v2 on v1

--- a/solution.py
+++ b/solution.py
@@ -12,6 +12,7 @@
 TWO_PI_RADIANS = 2.0 * math.pi
 LANES = 128
 DEPTH = 12
+MESH = pl.DeviceIdType.MESH
 
 
 def point_trig(node_phases):
@@ -75,47 +76,188 @@
     return (coefficient_actual, coefficient_image)
 
 
+def relatives(panel):
+    core, east, north = panel % 2, (panel // 2) % 2, panel // 4
+    return panel + 1 - 2 * core, panel + 2 - 4 * east, panel + 4 - 8 * north
+
+
+def gather_kernel(own_ref, out_ref, send_far, send_x, send_y, send_on, send_core, recv, local):
+    group, panel = lax.axis_index("group"), lax.axis_index("panel")
+    groups = lax.axis_size("group")
+    part = own_ref.shape[1]
+    core = panel % 2
+    mate, east, north = relatives(panel)
+    across = relatives(east)[2]
+    forward_from = north + core * (east - north)
+    forward_to = east + core * (north - east)
+
+    def slot(p, g):
+        return out_ref.at[p, :, pl.ds(g * part, part)]
+
+    def copy(p, g, send_sem, target, source=None):
+        return pltpu.make_async_remote_copy(
+            src_ref=slot(p, g) if source is None else source,
+            dst_ref=slot(p, g),
+            send_sem=send_sem,
+            recv_sem=recv.at[p, g],
+            device_id=target,
+            device_id_type=MESH,
+        )
+
+    def arrive(p, g):
+        copy(p, g, send_far.at[0], (group, mate)).wait_recv()
+
+    barrier = pltpu.get_barrier_semaphore()
+    peers = [(group, mate), (group, east), (group, north)]
+    peers += [(lax.rem(group + d, groups), panel) for d in range(1, groups)]
+    for peer in peers:
+        pl.semaphore_signal(barrier, inc=1, device_id=peer, device_id_type=MESH)
+    keep = pltpu.make_async_copy(own_ref, slot(panel, group), local)
+    keep.start()
+    pl.semaphore_wait(barrier, len(peers))
+    sent = []
+
+    def send(*args):
+        sent.append(copy(*args))
+        sent[-1].start()
+
+    for d in range(1, groups):
+        send(panel, group, send_far.at[d - 1], (lax.rem(group + d, groups), panel), own_ref)
+    order = [lax.rem(group + d, groups) for d in range(groups)]
+    for d, g in enumerate(order):
+        source = own_ref if d == 0 else None
+        if d:
+            arrive(panel, g)
+        send(panel, g, send_x.at[d], (group, east), source)
+        send(panel, g, send_y.at[d], (group, north), source)
+        send(panel, g, send_core.at[0, d], (group, mate), source)
+        arrive(forward_from, g)
+        send(forward_from, g, send_on.at[d], (group, forward_to))
+        send(forward_from, g, send_core.at[1, d], (group, mate))
+        arrive(forward_to, g)
+        send(forward_to, g, send_core.at[2, d], (group, mate))
+    for d, g in enumerate(order):
+        arrive(across, g)
+        send(across, g, send_core.at[3, d], (group, mate))
+    for p in (mate,) + relatives(mate)[1:] + (relatives(across)[0],):
+        for g in order:
+            arrive(p, g)
+    for item in sent:
+        item.wait_send()
+    keep.wait()
+
+
+def gather(own, groups, panels):
+    part = own.shape[1]
+    any_space = pl.BlockSpec(memory_space=pl.ANY)
+    dma = pltpu.SemaphoreType.DMA
+    return pl.pallas_call(
+        gather_kernel,
+        out_shape=jax.ShapeDtypeStruct(
+            (panels, own.shape[0], groups * part) + own.shape[2:], own.dtype
+        ),
+        in_specs=[any_space],
+        out_specs=any_space,
+        scratch_shapes=[
+            dma((groups - 1,)), dma((groups,)), dma((groups,)), dma((groups,)),
+            dma((4, groups)), dma((panels, groups)), dma,
+        ],
+        compiler_params=pltpu.CompilerParams(collective_id=0, has_side_effects=True),
+    )(own)
+
+
+def exchange_kernel(part_ref, out_ref, send, recv, local):
+    group, panel = lax.axis_index("group"), lax.axis_index("panel")
+    groups = lax.axis_size("group")
+    part = out_ref.shape[2]
+    barrier = pltpu.get_barrier_semaphore()
+    peers = [lax.rem(group + d, groups) for d in range(1, groups)]
+    for peer in peers:
+        pl.semaphore_signal(barrier, inc=1, device_id=(peer, panel), device_id_type=MESH)
+    keep = pltpu.make_async_copy(part_ref.at[:, pl.ds(group * part, part)], out_ref.at[0], local)
+    keep.start()
+    pl.semaphore_wait(barrier, len(peers))
+    copies = [
+        pltpu.make_async_remote_copy(
+            src_ref=part_ref.at[:, pl.ds(peer * part, part)],
+            dst_ref=out_ref.at[d + 1],
+            send_sem=send.at[d],
+            recv_sem=recv.at[d],
+            device_id=(peer, panel),
+            device_id_type=MESH,
+        )
+        for d, peer in enumerate(peers)
+    ]
+    for copy in copies:
+        copy.start()
+    for copy in copies:
+        copy.wait()
+    keep.wait()
+
+
+def exchange(parts, groups):
+    any_space = pl.BlockSpec(memory_space=pl.ANY)
+    dma = pltpu.SemaphoreType.DMA
+    slots, rows = parts.shape[0], parts.shape[1]
+    return pl.pallas_call(
+        exchange_kernel,
+        out_shape=jax.ShapeDtypeStruct(
+            (groups, slots, rows // groups) + parts.shape[2:], parts.dtype
+        ),
+        in_specs=[any_space],
+        out_specs=any_space,
+        scratch_shapes=[dma((groups - 1,)), dma((groups - 1,)), dma],
+        compiler_params=pltpu.CompilerParams(collective_id=1, has_side_effects=True),
+    )(parts)
+
+
 def product_kernel(
-    count_ref, order_ref, trig_ref, weight_ref, a_ref, spread_ref, b_ref, out_ref, buf, acc, sems
+    count_ref, order_ref, trig_ref, weight_ref, whole_ref, spread_ref, share_ref, out_ref,
+    a_ref, buf, acc, total_ref, sems, a_sems, out_sem,
 ):
-    rows, inner = a_ref.shape[1], a_ref.shape[2]
-    tiles = b_ref.shape[2]
-    depth, _, kb = buf.shape[0], buf.shape[1], buf.shape[2]
-    blocks = inner // kb
+    blocks, pieces, rows, kb = a_ref.shape
+    depth, cols = buf.shape[0], buf.shape[2]
+    b_ref = share_ref.reshape(share_ref.shape[0], 2 * blocks * kb, cols)
     total = count_ref[0] * blocks
 
-    def copies(step):
-        point = order_ref[step // blocks]
-        start = pl.multiple_of((step % blocks) * kb, kb)
+    def copy(step):
+        start = pl.multiple_of((step % blocks) * 2 * kb, 2 * kb)
         slot = step % depth
-        return [
-            pltpu.make_async_copy(
-                b_ref.at[point, pl.ds(start, kb), t], buf.at[slot, t], sems.at[slot, t]
-            )
-            for t in range(tiles)
-        ]
+        return pltpu.make_async_copy(
+            b_ref.at[order_ref[step // blocks], pl.ds(start, 2 * kb)], buf.at[slot], sems.at[slot]
+        )
+
+    def take(block):
+        return pltpu.make_async_copy(
+            whole_ref.at[block].reshape(pieces, rows, kb), a_ref.at[block], a_sems.at[block]
+        )
 
     def fetch(step):
         @pl.when(step < total)
         def _():
-            for copy in copies(step):
-                copy.start()
-
-    for step in range(depth - 1):
+            copy(step).start()
+
+    fetch(0)
+    for block in range(blocks):
+        take(block).start()
+    for step in range(1, depth - 1):
         fetch(step)
-    out_ref[...] = jnp.zeros_like(out_ref)
+    total_ref[...] = jnp.zeros_like(total_ref)
+    for block in range(blocks):
+        take(block).wait()
 
     def body(step, carry):
         fetch(step + depth - 1)
+        copy(step).wait()
         point = order_ref[step // blocks]
         block = step % blocks
-        start = pl.multiple_of(block * kb, kb)
+        slot = step % depth
         real = jnp.zeros((rows, kb), jnp.float32)
         imag = jnp.zeros((rows, kb), jnp.float32)
-        for e in range(a_ref.shape[0]):
-            piece = a_ref[e, :, pl.ds(start, kb)].astype(jnp.float32)
+        for e in range(pieces):
+            piece = a_ref[block, e].astype(jnp.float32)
             real = real + piece * trig_ref[point, e]
-            imag = imag + piece * trig_ref[point, a_ref.shape[0] + e]
+            imag = imag + piece * trig_ref[point, pieces + e]
         real = real.astype(jnp.bfloat16)
         imag = imag.astype(jnp.bfloat16)
         parts = []
@@ -130,56 +272,57 @@
         left = jnp.concatenate(
             [mixed[2 * rows * t : 2 * rows * (t + 1)] for t in range(kb // LANES)], axis=1
         )
-        for copy in copies(step):
-            copy.wait()
-        slot = step % depth
-        right = jnp.concatenate(
-            [buf[slot, t].reshape(2 * kb, LANES) for t in range(tiles)], axis=1
-        )
-        product = jnp.dot(left, right, preferred_element_type=jnp.float32)
-        value = jnp.where(block == 0, product, acc[...] + product)
-        acc[...] = value
+        product = jnp.dot(left, buf[slot], preferred_element_type=jnp.float32)
+        acc[...] = jnp.where(block == 0, product, acc[...] + product)
 
         @pl.when(block == blocks - 1)
         def _():
             for e in range(4):
-                out_ref[e] += (
-                    weight_ref[point, e] * value[:rows] - weight_ref[point, 4 + e] * value[rows:]
+                total_ref[e] += (
+                    weight_ref[point, e] * acc[:rows] - weight_ref[point, 4 + e] * acc[rows:]
                 )
 
         return carry
 
     lax.fori_loop(0, total, body, 0)
+    done = pltpu.make_async_copy(total_ref, out_ref.reshape(*total_ref.shape), out_sem)
+    done.start()
+    done.wait()
 
 
 def weighted_product(count, order, trig, weight, whole, shares):
-    here, inner, tiles = shares.shape[0], shares.shape[1], shares.shape[2]
-    rows = whole.shape[1]
-    kb = min(inner, 512)
+    cols = shares.shape[3]
+    blocks, pieces, row_tiles, tile, kb = whole.shape
+    rows = row_tiles * tile
     index = jnp.arange(2 * LANES)
     target = jnp.where(index < LANES, 2 * index, 2 * (index - LANES) + 1)
     spread = (target[:, None] == index[None, :]).astype(jnp.bfloat16)
     smem = pl.BlockSpec(memory_space=pltpu.SMEM)
-    vmem = pl.BlockSpec(memory_space=pltpu.VMEM)
+    any_space = pl.BlockSpec(memory_space=pl.ANY)
     return pl.pallas_call(
         product_kernel,
-        out_shape=jax.ShapeDtypeStruct((4, rows, tiles * LANES), jnp.float32),
-        in_specs=[smem, smem, smem, smem, vmem, vmem, pl.BlockSpec(memory_space=pl.ANY)],
-        out_specs=vmem,
+        out_shape=jax.ShapeDtypeStruct((4, row_tiles, tile, cols), jnp.float32),
+        in_specs=[
+            smem, smem, smem, smem, any_space, pl.BlockSpec(memory_space=pltpu.VMEM), any_space,
+        ],
+        out_specs=any_space,
         scratch_shapes=[
-            pltpu.VMEM((DEPTH, tiles, kb, 2, LANES), jnp.bfloat16),
-            pltpu.VMEM((2 * rows, tiles * LANES), jnp.float32),
-            pltpu.SemaphoreType.DMA((DEPTH, tiles)),
+            pltpu.VMEM((blocks, pieces, rows, kb), jnp.bfloat16),
+            pltpu.VMEM((DEPTH, 2 * kb, cols), jnp.bfloat16),
+            pltpu.VMEM((2 * rows, cols), jnp.float32),
+            pltpu.VMEM((4, rows, cols), jnp.float32),
+            pltpu.SemaphoreType.DMA((DEPTH,)),
+            pltpu.SemaphoreType.DMA((blocks,)),
+            pltpu.SemaphoreType.DMA,
         ],
         compiler_params=pltpu.CompilerParams(vmem_limit_bytes=50 << 20),
     )(count, order, trig, weight, whole, spread, shares)
 
 
-def shards(source_matrix_tiles, second_operand_encoded, responding_nodes):
+def shards(own_kernels, groups, panels, source_matrix_tiles, shares, responding_nodes):
     coefficient_actual, coefficient_image = recovery_coefficients(responding_nodes)
-    here, inner, _, cols = second_operand_encoded.shape
-    first_point = lax.axis_index("group") * here
-    points = first_point + jnp.arange(here, dtype=jnp.int32)
+    here, cols = shares.shape[0], shares.shape[3]
+    points = lax.axis_index("group") * here + jnp.arange(here, dtype=jnp.int32)
     selector = (responding_nodes[:, None] == points[None, :]).astype(jnp.float32)
     highest = lax.Precision.HIGHEST
     weight = jnp.concatenate(
@@ -190,29 +333,35 @@
         axis=1,
     )
     listed = jnp.any(responding_nodes[:, None] == points[None, :], axis=0)
-    rank = jnp.cumsum(listed.astype(jnp.int32)) - 1
     local = jnp.arange(here, dtype=jnp.int32)
+    rank = jnp.sum((local[None, :] < local[:, None]) & listed[None, :], axis=1)
     order = jnp.sum(
         jnp.where(listed[None, :] & (rank[None, :] == local[:, None]), local[None, :], 0), axis=1
     )
     count = jnp.sum(listed.astype(jnp.int32))[None]
     trig = point_trig(TWO_PI_RADIANS * points.astype(jnp.float32) / NODE_NUMBER)
     trig = trig.reshape(here, 16)
-    whole = lax.all_gather(source_matrix_tiles, "group", axis=1, tiled=True)
-    whole = lax.all_gather(whole, "panel", axis=3, tiled=True)
-    rows = whole.shape[1]
-    whole = whole.transpose(0, 2, 1, 3).reshape(8, rows, inner)
-    shares = second_operand_encoded.reshape(here, inner, 2, cols // LANES, LANES)
-    shares = shares.transpose(0, 1, 3, 2, 4)
-    partial_sum = weighted_product(count, order, trig, weight, whole, shares)
-    partial_sum = partial_sum.reshape(2, 2, rows, cols).transpose(0, 2, 1, 3)
-    return lax.psum_scatter(partial_sum, "group", scatter_dimension=1, tiled=True)
+    _, rows, _, kb = source_matrix_tiles.shape
+    tile = math.gcd(rows, 4)
+    own = source_matrix_tiles.transpose(0, 2, 1, 3).reshape(8, rows // tile, tile, kb)
+    if own_kernels:
+        whole = gather(own, groups, panels)
+    else:
+        whole = lax.all_gather(own, "group", axis=1, tiled=True)
+        whole = lax.all_gather(whole, "panel", axis=0)
+    parts = weighted_product(count, order, trig, weight, whole, shares)
+    if own_kernels:
+        result = jnp.sum(exchange(parts, groups), axis=0)
+    else:
+        result = lax.psum_scatter(parts, "group", scatter_dimension=1, tiled=True)
+    return result.reshape(2, 2, rows, cols).transpose(0, 2, 1, 3)
 
 
 def solution(mesh):
     placed = (P(None, "group", None, "panel"), P("group", None, None, "panel"), P())
+    groups, panels = mesh.shape["group"], mesh.shape["panel"]
     return jax.shard_map(
-        shards,
+        functools.partial(shards, panels == 8, groups, panels),
         mesh=mesh,
         in_specs=placed,
         out_specs=P(None, "group", None, "panel"),

time: 156 us -> 79.6 us (0.51)
  waiting for transfers between devices: 77.6 us -> 0 us
  Pallas kernels: 33.2 us -> 65.5 us
  blocking collectives: 18.4 us -> 0 us
  between operations: 14.2 us -> 0.15 us
  local copies, waits for them, and re-layouts: 6.87 us -> 5.05 us
  other arithmetic: 3.5 us -> 5.11 us
    unnamed x3 -> x0, waiting for transfers between devices: 50.2 us -> none
    pallas_call x1 -> x3, Pallas kernels: 33.2 us -> 65.5 us  [the longest x1 31.3 us: gather(): pl.pallas_call(gather_kernel, out_shape=jax.ShapeDtypeStruct((panels, own...]
    all_gather x1 -> x0, waiting for transfers between devices: 27.3 us -> none  [shards(): whole = lax.all_gather(whole, 'panel', axis=3, tiled=True)]
    all_gather x1 -> x0, blocking collectives: 18.4 us -> none  [shards(): whole = lax.all_gather(source_matrix_tiles, 'group', axis=1, tiled=True)]
    transpose x1, local copies, waits for them, and re-layouts: 3.61 us -> 0.65 us  [shards(): return result.reshape(2, 2, rows, cols).transpose(0, 2, 1, 3)]
  transfers between devices with their start and end apart: 2 -> 0, of which waited for: 2 -> 0; matrix products, arithmetic and copies ran while one was open for 4% -> 0% of each run, Pallas kernels for 0% -> 0%
where the time goes in v2:
time: 79.6 us; the launch traced here: 78.8 us
  Pallas kernels  65.5 us (82%)
  other arithmetic  5.11 us (6%)
  local copies, waits for them, and re-layouts  5.05 us (6%)
  matrix products  3.04 us (4%)
    pallas_call x1, Pallas kernels, gather(): pl.pallas_call(gather_kernel, out_shape=jax.ShapeDtypeStruct((panels, own...  31.3 us
    pallas_call x1, Pallas kernels, weighted_product(): pl.pallas_call(product_kernel, out_shape=jax.ShapeDtypeStruct((4, row_til...  21 us
    pallas_call x1, Pallas kernels, exchange(): pl.pallas_call(exchange_kernel, out_shape=jax.ShapeDtypeStruct((groups, s...  13.1 us
    unnamed x4, local copies, waits for them, and re-layouts  2.61 us
    reshape x2, local copies, waits for them, and re-layouts, shards(): source_matrix_tiles.transpose(0, 2, 1, 3).reshape(8, rows // tile, tile, kb)  1.6 us

profile of v2, /device:TPU:0, one launch (start us, length us, event | category | flops | bytes accessed | tf_op | source)
XLA Modules:
  0.0 78.8 jit_solution(17788857418085793632)
XLA Ops:
  0.0 0.8 %compare_reduce_fusion = pred[8]{0:T(512)(128)(4,1)S(1)} fusion(s32[19]{0:T(128)} %param.5, s32[8]{0:T(128)S(1)} %iota_add_fusion.2), kind=kLoop, calls=%fused_computation.45 | loop fusion | flops 296 | bytes 116 | tf_op jit(solution)/shard_map/reduce_or | solution.py:335
  0.9 0.6 convert_reduce_fusion.1
  1.5 0.1 convert_reduce_fusion
  1.6 0.1 select_reduce_fusion.order_ref
  1.7 0.1 iota_add_fusion.1
  1.9 0.7 fusion.48
  2.6 0.1 multiply_cosine_fusion.3
  2.7 0.1 copy.88.trig_ref
  2.8 0.1 broadcast_subtract_fusion
  2.9 0.1 fusion.spread_ref
  3.0 0.9 %copy.93 = bf16[2,4,12,512]{3,2,1,0:T(8,128)(2,1)S(1)} copy(bf16[2,4,12,512]{3,1,2,0:T(4,128)(2,1)} %bitcast.23) | data formatting | bytes 196608 | tf_op jit(solution)/shard_map/reshape | solution.py:346
  3.9 0.7 reshape.163.own_ref
  4.6 0.1 broadcast_select_fusion.1
  4.9 0.8 %fusion.8 = (f32[19]{0:T(128)S(1)}, f32[19]{0:T(128)S(1)}, f32[19,1,32]{2,0,1:T(8,128)S(1)}, f32[19,1,32]{2,0,1:T(8,128)S(1)}) fusion(s32[19]{0:T(128)} %param.5, f32[19,2,32]{2,0,1:T(8,128)S(1)} %get-tuple-element.16, f32[19,2,32]{2,0,1:T(8,128)S(1)} %get-tuple-element.15), kind=kLoop, calls=%fused_computation.27 | loop fusion | flops 6650 | bytes 14820 | tf_op jit(solution)/shard_map/reduce_sum | solution.py:67
  5.7 0.3 fusion.2
  6.0 0.3 fusion.1
  6.4 0.3 convolution_subtract_fusion
  6.7 0.3 convolution_add_fusion
  7.0 0.8 %fusion.17 = f32[8,4]{1,0:T(8,128)S(1)} fusion(f32[19,4]{0,1:T(4,128)S(1)} %convolution_subtract_fusion, f32[19,4]{0,1:T(4,128)S(1)} %convolution_add_fusion, s32[19]{0:T(128)} %param.5, s32[8]{0:T(128)S(1)} %iota_add_fusion.2, f32[19]{0:T(128)S(1)} %get-tuple-element.22, f32[19]{0:T(128)S(1)} %get-tuple-element.23, f32[19]{0:T(128)S(1)} %get-tuple-element.21), kind=kOutput, calls=%fused_computation.41 | convolution fusion | flops 7752 | bytes 1072 | tf_op jit(solution)/shard_map/dot_general | solution.py:331
  7.9 0.8 %fusion.19 = f32[8,4]{1,0:T(8,128)S(1)} fusion(f32[19,4]{0,1:T(4,128)S(1)} %convolution_add_fusion, f32[19,4]{0,1:T(4,128)S(1)} %convolution_subtract_fusion, s32[19]{0:T(128)} %param.5, s32[8]{0:T(128)S(1)} %iota_add_fusion.2, f32[19]{0:T(128)S(1)} %get-tuple-element.22, f32[19]{0:T(128)S(1)} %get-tuple-element.23, f32[19]{0:T(128)S(1)} %get-tuple-element.21), kind=kOutput, calls=%fused_computation.43 | convolution fusion | flops 7752 | bytes 1072 | tf_op jit(solution)/shard_map/dot_general | solution.py:330
  8.7 0.1 pad_maximum_fusion.1.weight_ref
  8.8 31.3 %shard_map.37.whole_ref = bf16[8,8,12,4,512]{4,3,2,1,0:T(4,128)(2,1)} custom-call(bf16[8,3,4,512]{3,2,1,0:T(4,128)(2,1)} %reshape.163.own_ref), custom_call_target="tpu_custom_call" | custom-call | tf_op jit(solution)/shard_map/pallas_call | solution.py:154
  40.1 0.0 copy-start
  40.1 1.9 %copy-done = bf16[8,8,12,4,512]{4,3,2,1,0:T(4,128)(2,1)S(1)} copy-done((bf16[8,8,12,4,512]{4,3,2,1,0:T(4,128)(2,1)S(1)}, bf16[8,8,12,4,512]{4,3,2,1,0:T(4,128)(2,1)}, u32[]{:S(2)}) %copy-start) | copy-done | bytes 3145752
  42.0 21.0 %shard_map.38.part_ref = f32[4,12,4,512]{3,2,1,0:T(4,128)S(1)} custom-call(s32[1]{0:T(128)} %bitcast.count_ref, s32[8]{0:T(128)S(1)} %select_reduce_fusion.order_ref, f32[8,16]{1,0:T(8,128)S(1)} %copy.88.trig_ref, f32[8,8]{1,0:T(8,128)S(1)} %pad_maximum_fusion.1.weight_ref, bf16[8,8,12,4,512]{4,3,2,1,0:T(4,128)(2,1)S(1)} %copy-done, ...), custom_call_target="tpu_custom_call" | custom-call | tf_op jit(solution)/shard_map/pallas_call | solution.py:302
  63.0 0.0 copy-start.1
  63.1 0.7 copy-done.1
  63.8 13.1 %shard_map.39 = f32[4,4,3,4,512]{4,3,2,1,0:T(4,128)} custom-call(f32[4,12,4,512]{3,2,1,0:T(4,128)} %copy-done.1), custom_call_target="tpu_custom_call" | custom-call | tf_op jit(solution)/shard_map/pallas_call | solution.py:202
  76.9 1.1 %reduce_sum.59 = f32[4,3,4,512]{3,2,1,0:T(4,128)S(1)} reduce(f32[4,4,3,4,512]{4,3,2,1,0:T(4,128)} %shard_map.39, f32[]{:T(128)} %constant.13.clone.1), dimensions={0}, to_apply=%region_6.7 | reduce | flops 73728 | bytes 491524 | tf_op jit(solution)/shard_map/reduce_sum | solution.py:354
  78.1 0.1 reshape.162
  78.2 0.6 copy.90
  (16 shorter events, 0.3 us)
Async XLA Ops:
  40.1 1.9 %copy-start = (bf16[8,8,12,4,512]{4,3,2,1,0:T(4,128)(2,1)S(1)}, bf16[8,8,12,4,512]{4,3,2,1,0:T(4,128)(2,1)}, u32[]{:S(2)}) copy-start(bf16[8,8,12,4,512]{4,3,2,1,0:T(4,128)(2,1)} %shard_map.37.whole_ref) | copy-start | bytes 9437188
  63.0 0.7 copy-start.1
